TPU v7x, 256 devices: a whole 4x4x8 slice. The times are simulated.
256 devices in a mesh: leaf: 32 (over x_hi, z, core), head: 8 (over x_lo, y).
Axes of the slice: x: 4 (x_hi: 2, x_lo: 2; x = x_hi * 2 + x_lo), y: 4, z: 8, core: 2. Of those that a mesh axis runs over, the one named last changes fastest.
Arguments:
- latents: bfloat16 [2048, 512], P('leaf'), may hold values from -14 to 14
- queries: bfloat16 [4096, 64, 128], P('leaf', 'head'), may hold values from -14 to 14
- grad_out: bfloat16 [4096, 64, 128], P('leaf', 'head'), may hold values from -6 to 6
- key_up_matrix: bfloat16 [64, 128, 512], P('head'), may hold values from -0.25 to 0.25
- value_up_matrix: bfloat16 [64, 512, 128], P('head'), may hold values from -0.25 to 0.25
- parents: int32 [256], replicated, may hold values from 0 to 254, as said below
- branch_node: int32 [32, 8], P('leaf'), may hold values from 0 to 255
- branch_lengths: int32 [32, 8], P('leaf'), may hold values from 1 to 40, 128 in all within a row
Outputs:
- d_queries: bfloat16 [4096, 64, 128], P('leaf', 'head')
- d_latents: float32 [2048, 512], P('leaf')
Inputs may be any that keep to these rules, and one draw needn't show every extreme that they name: parents[0] = 0 and parents[n] < n for every n >= 1.
All inputs are finite; a program needn't handle non-finite values.
Results may differ from a plain program's by a relative error of at most 0.025.
The roundings to bfloat16 on the way count: a program that leaves them out, or rounds other values in their place, can miss the bound.
Values may be sent and summed in bfloat16 or wider, within the bound.
A program may use at most 64 MiB of HBM per device.

v0:
```python
import jax
import jax.numpy as jnp
from jax import lax
from jax.sharding import PartitionSpec as P

NODE_LEN = 8
softmax_scale = 192.0 ** (-0.5)
masked_score = -1e30


def ancestry(parents):
    node_count = parents.shape[0]
    indices = jnp.arange(node_count, dtype=jnp.int32)
    linked = (parents[:, None] == indices[None, :]) | (indices[:, None] == indices[None, :])
    closure = linked.astype(jnp.float32)
    for squaring in range(node_count.bit_length()):
        closure = jnp.minimum(jnp.dot(closure, closure, precision=lax.Precision.HIGHEST), 1.0)
    return closure


def token_nodes(lengths_row, nodes_row, tok_count):
    bounds = jnp.cumsum(lengths_row)
    places = jnp.arange(tok_count, dtype=jnp.int32)
    branch_of = jnp.sum((places[:, None] >= bounds[None, :]).astype(jnp.int32), axis=1)
    select = branch_of[:, None] == jnp.arange(lengths_row.shape[0], dtype=jnp.int32)[None, :]
    return jnp.sum(jnp.where(select, nodes_row[None, :], 0), axis=1)


def live_keys(node_list, closure):
    node_count = closure.shape[0]
    select = (node_list[:, None] == jnp.arange(node_count, dtype=jnp.int32)[None, :]).astype(
        jnp.float32
    )
    reached = jnp.dot(select, closure, precision=lax.Precision.HIGHEST) > 0.5
    return jnp.repeat(reached, NODE_LEN, axis=1)


def on_device(
    latents, queries, grad_out, key_up_matrix, value_up_matrix, parents, branch_node, branch_lengths
):
    closure = ancestry(parents)
    tok_count = queries.shape[0]
    heads_here = queries.shape[1]
    width = latents.shape[1]
    node_list = token_nodes(branch_lengths[0], branch_node[0], tok_count)
    key_live = live_keys(node_list, closure)
    prefix_rows = key_live.shape[1]
    query_latent = jnp.einsum(
        "thd,hdc->thc", queries, key_up_matrix, preferred_element_type=jnp.float32
    ).astype(jnp.bfloat16)
    grad_latent = jnp.einsum(
        "thv,hcv->thc", grad_out, value_up_matrix, preferred_element_type=jnp.float32
    ).astype(jnp.bfloat16)

    def scores(block_keys):
        usable = key_live[:, None, :]
        scaled = (
            jnp.einsum("thc,kc->thk", query_latent, block_keys, preferred_element_type=jnp.float32)
            * softmax_scale
        )
        return (usable, jnp.where(usable, scaled, masked_score))

    forward_start = (
        jnp.full((tok_count, heads_here), masked_score, jnp.float32),
        jnp.zeros((tok_count, heads_here), jnp.float32),
        jnp.zeros((tok_count, heads_here, width), jnp.float32),
    )
    block_keys = lax.all_gather(latents, "leaf", axis=0, tiled=True)

    def advance(state):
        running_max, running_sum, weighted = state
        usable, logits = scores(block_keys)
        new_max = jnp.maximum(running_max, jnp.max(logits, axis=-1))
        weights = jnp.where(usable, jnp.exp(logits - new_max[..., None]), 0.0)
        weighted = jnp.einsum(
            "thk,kc->thc",
            weights.astype(jnp.bfloat16),
            block_keys,
            preferred_element_type=jnp.float32,
        )
        return (new_max, jnp.sum(weights, axis=-1), weighted)

    running_max, running_sum, weighted = advance(forward_start)
    attended = weighted / running_sum[..., None]
    log_norm = running_max + jnp.log(running_sum)
    delta = jnp.sum(grad_latent.astype(jnp.float32) * attended, axis=-1)
    backward_start = (
        jnp.zeros((tok_count, heads_here, width), jnp.float32),
        jnp.zeros((prefix_rows, width), jnp.float32),
    )
    backward_block_keys = lax.all_gather(latents, "leaf", axis=0, tiled=True)

    def advance(state):
        usable, logits = scores(backward_block_keys)
        probs = jnp.where(usable, jnp.exp(logits - log_norm[..., None]), 0.0)
        grad_weights = jnp.einsum(
            "thc,kc->thk", grad_latent, backward_block_keys, preferred_element_type=jnp.float32
        )
        grad_scores = (probs * (grad_weights - delta[..., None])).astype(jnp.bfloat16)
        query_acc = jnp.einsum(
            "thk,kc->thc", grad_scores, backward_block_keys, preferred_element_type=jnp.float32
        )
        contrib = softmax_scale * jnp.einsum(
            "thk,thc->kc", grad_scores, query_latent, preferred_element_type=jnp.float32
        )
        contrib = contrib + jnp.einsum(
            "thk,thc->kc",
            probs.astype(jnp.bfloat16),
            grad_latent,
            preferred_element_type=jnp.float32,
        )
        return (query_acc, contrib)

    query_acc, latent_grad = advance(backward_start)
    query_grad = (softmax_scale * query_acc).astype(jnp.bfloat16)
    d_queries = jnp.einsum(
        "thc,hdc->thd", query_grad, key_up_matrix, preferred_element_type=jnp.float32
    ).astype(jnp.bfloat16)
    owned_rows = lax.psum_scatter(
        latent_grad.astype(jnp.bfloat16), "leaf", scatter_dimension=0, tiled=True
    )
    d_latents = lax.psum(owned_rows, "head").astype(jnp.float32)
    return (d_queries, d_latents)


def solution(mesh):
    placed = (
        P("leaf", None),
        P("leaf", "head", None),
        P("leaf", "head", None),
        P("head", None, None),
        P("head", None, None),
        P(),
        P("leaf", None),
        P("leaf", None),
    )
    return jax.shard_map(
        on_device,
        mesh=mesh,
        in_specs=placed,
        out_specs=(P("leaf", "head", None), P("leaf", None)),
        check_vma=False,
    )
```

profile of v0, /device:TPU:4, one launch (start us, length us, event | category | flops | bytes accessed | tf_op | source)
XLA Modules:
  0.0 321.0 jit_solution(14642406166411518721)
XLA Ops:
  7.2 0.7 all-gather.2.cloned.1.call-update
  8.0 0.8 reduce-window.8
  8.8 0.1 convert_reduce_fusion
  8.9 0.7 select_reduce_fusion
  9.6 1.0 convolution_minimum_fusion.8
  10.7 0.4 convolution_minimum_fusion.7
  11.1 0.4 convolution_minimum_fusion.6
  11.4 0.4 convolution_minimum_fusion.5
  11.8 0.4 convolution_minimum_fusion.4
  12.2 0.4 convolution_minimum_fusion.3
  12.6 0.4 convolution_minimum_fusion.2
  13.0 0.4 convolution_minimum_fusion.1
  13.4 0.4 convolution_minimum_fusion
  13.8 0.3 convolution_compare_fusion
  14.0 0.1 copy.34
  14.2 0.1 broadcast_bitcast_fusion
  14.3 0.4 copy.35
  14.7 1.5 fusion.23
  16.2 2.4 fusion.24
  18.6 72.7 %all-gather.2.cloned.1.call-done = bf16[2048,512]{1,0:T(8,128)(2,1)} async-done(((bf16[64,512]{1,0:T(8,128)(2,1)}), bf16[2048,512]{1,0:T(8,128)(2,1)}) %all-gather.2.cloned.1.call-update) | async-done | bytes 2097168 | tf_op jit(solution)/shard_map/all_gather | solution.py:91
  91.3 4.5 %fusion.3 = (f32[128,8]{0,1:T(8,128)S(1)}, f32[128,8,2048]{2,0,1:T(8,128)S(1)}) fusion(pred[128,2048]{1,0:T(8,128)(4,1)S(1)} %copy.35, bf16[128,8,512]{0,2,1:T(8,128)(2,1)S(1)} %fusion.23, bf16[2048,512]{1,0:T(8,128)(2,1)} %all-gather.2.cloned.1.call-done), kind=kOutput, calls=%fused_computation.7 | convolution fusion | flops 2153774080 | bytes 11800576 | tf_op jit(solution)/shard_map/thc,kc->thk/dot_general | solution.py:58
  95.8 2.7 fusion.1
  98.5 3.3 %fusion.4 = f32[2048,512,1]{1,0,2:T(8,128)S(1)} fusion(bf16[128,8,512]{0,2,1:T(8,128)(2,1)S(1)} %copy-done.2, f32[128,8,2048]{2,0,1:T(8,128)S(1)} %get-tuple-element.9, f32[128,8]{0,1:T(8,128)S(1)} %log_add_fusion, pred[128,2048]{1,0:T(8,128)(4,1)S(1)} %copy.35), kind=kOutput, calls=%fused_computation.8 | convolution fusion | flops 2157969408 | bytes 13897728 | tf_op jit(solution)/shard_map/thk,thc->kc/dot_general | solution.py:106
  101.8 2.8 multiply_reduce_fusion
  104.6 5.5 %multiply_convert_fusion = bf16[128,8,2048]{2,0,1:T(8,128)(2,1)S(1)} fusion(f32[128,8,2048]{2,0,1:T(8,128)S(1)} %get-tuple-element.9, f32[128,8]{0,1:T(8,128)S(1)} %multiply_reduce_fusion, f32[128,8]{0,1:T(8,128)S(1)} %log_add_fusion, pred[128,2048]{1,0:T(8,128)(4,1)S(1)} %copy.35, bf16[128,8,512]{0,2,1:T(8,128)(2,1)S(1)} %copy-done.2, ...), kind=kOutput, calls=%fused_computation | convolution fusion | flops 2162163712 | bytes 15998976 | tf_op jit(solution)/shard_map/thc,kc->thk/dot_general | solution.py:96
  110.1 1.9 copy-done.4
  112.0 4.0 %fusion.6 = bf16[2048,512]{1,0:T(8,128)(2,1)} fusion(f32[2048,512,1]{1,0,2:T(8,128)S(1)} %fusion.4, bf16[128,8,2048]{2,0,1:T(8,128)(2,1)S(1)} %multiply_convert_fusion, bf16[128,8,512]{0,2,1:T(8,128)(2,1)S(1)} %fusion.23), kind=kOutput, calls=%fused_computation.10 | convolution fusion | flops 2150629376 | bytes 11534336 | tf_op jit(solution)/shard_map/thk,thc->kc/dot_general | solution.py:103
  116.1 117.2 %reduce-scatter.2.cloned.1.call-done = bf16[64,512]{1,0:T(8,128)(2,1)} async-done(((bf16[2048,512]{1,0:T(8,128)(2,1)}), bf16[64,512]{1,0:T(8,128)(2,1)}) %reduce-scatter.2.cloned.1.call-update) | async-done | bytes 65552 | tf_op jit(solution)/shard_map/reduce_scatter | solution.py:119
  233.3 5.5 %fusion.31 = bf16[128,8,128]{2,0,1:T(8,128)(2,1)S(1)} fusion(bf16[8,128,512]{2,1,0:T(8,128)(2,1)S(1)} %copy-done, bf16[128,8,2048]{2,0,1:T(8,128)(2,1)} %copy-done.4, bf16[2048,512]{1,0:T(8,128)(2,1)} %all-gather.2.cloned.1.call-done), kind=kOutput, calls=%fused_computation.42 | convolution fusion | flops 2282881024 | bytes 7602176 | tf_op jit(solution)/shard_map/thc,hdc->thd/dot_general | solution.py:116
  238.8 0.9 copy.46
  239.6 73.3 %all-reduce.2.cloned.1.call-done = bf16[64,512]{1,0:T(8,128)(2,1)} async-done(((bf16[64,512]{1,0:T(8,128)(2,1)}), bf16[64,512]{1,0:T(8,128)(2,1)}) %all-reduce.2.cloned.1.call-update) | async-done | bytes 65552 | tf_op jit(solution)/shard_map/psum | solution.py:122
  313.0 1.5 convert_element_type.57
  (16 shorter events, 0.2 us)
Async XLA Ops:
  7.2 7.6 %copy-start = (bf16[8,128,512]{2,1,0:T(8,128)(2,1)S(1)}, bf16[8,128,512]{2,1,0:T(8,128)(2,1)}, u32[]{:S(2)}) copy-start(bf16[8,128,512]{2,1,0:T(8,128)(2,1)} %param.11) | copy-start | bytes 3145732
  7.2 9.0 %copy-start.1 = (bf16[8,512,128]{2,1,0:T(8,128)(2,1)S(1)}, bf16[8,512,128]{2,1,0:T(8,128)(2,1)}, u32[]{:S(2)}) copy-start(bf16[8,512,128]{2,1,0:T(8,128)(2,1)} %param.12) | copy-start | bytes 3145732
  7.2 84.1 %all-gather.2.cloned.1.call-start = ((), (), s32[]{:S(2)}) async-start(), calls=%async_computation.1 | async-start | bytes 2162688 | tf_op jit(solution)/shard_map/all_gather | solution.py:91
  7.9 225.3 %reduce-scatter.2.cloned.1.call-start = ((), (), s32[]{:S(2)}) async-start(), calls=%async_computation.2 | async-start | bytes 2162688 | tf_op jit(solution)/shard_map/reduce_scatter | solution.py:119
  18.6 79.9 %copy-start.2 = (bf16[128,8,512]{0,2,1:T(8,128)(2,1)S(1)}, bf16[128,8,512]{0,2,1:T(8,128)(2,1)}, u32[]{:S(2)}) copy-start(bf16[128,8,512]{0,2,1:T(8,128)(2,1)} %fusion.24) | copy-start | bytes 3145732
  98.5 3.3 %copy-start.3 = (bf16[2048,512]{1,0:T(8,128)(2,1)S(1)}, bf16[2048,512]{1,0:T(8,128)(2,1)}, u32[]{:S(2)}) copy-start(bf16[2048,512]{1,0:T(8,128)(2,1)} %all-gather.2.cloned.1.call-done) | copy-start | bytes 6291460
  110.1 1.9 copy-start.4
  116.0 196.9 %all-reduce.2.cloned.1.call-start = ((), (), s32[]{:S(2)}) async-start(), calls=%async_computation.3 | async-start | bytes 131072 | tf_op jit(solution)/shard_map/psum | solution.py:122
Sparse Core Ops, SparseCore 0:
  10.8 80.4 all-gather.1
  116.2 117.0 reduce-scatter.1
  236.1 76.8 all-reduce.1
where the time goes:
time: 321 us
  waiting for transfers between devices  264 us (82%)
  matrix products  33.7 us (10%)
  between operations  14 us (4%)
  other arithmetic  5.85 us (2%)
  local copies, waits for them, and re-layouts  3.47 us (1%)
    reduce_scatter x1, waiting for transfers between devices, on_device(): lax.psum_scatter(latent_grad.astype(jnp.bfloat16), 'leaf', scatter_dimens...  117 us
    psum x1, waiting for transfers between devices, on_device(): d_latents = lax.psum(owned_rows, 'head').astype(jnp.float32)  73.3 us
    all_gather x1, waiting for transfers between devices, on_device(): backward_block_keys = lax.all_gather(latents, 'leaf', axis=0, tiled=True)  72.7 us
  transfers between devices with their start and end apart: 3, of which 3 were waited for; matrix products, arithmetic and copies ran while one was open for 5% of the time, Pallas kernels for 0%

commit v1 on v0

--- a/solution.py
+++ b/solution.py
@@ -119,7 +119,7 @@
     owned_rows = lax.psum_scatter(
         latent_grad.astype(jnp.bfloat16), "leaf", scatter_dimension=0, tiled=True
     )
-    d_latents = lax.psum(owned_rows, "head").astype(jnp.float32)
+    d_latents = jnp.sum(lax.all_gather(owned_rows, "head"), axis=0).astype(jnp.float32)
     return (d_queries, d_latents)
 
 

time: 321 us -> 271 us (0.84)
  waiting for transfers between devices: 264 us -> 184 us
  blocking collectives: 0 us -> 29.1 us
    psum x1 -> x0, waiting for transfers between devices: 73.3 us -> none  [on_device(): d_latents = lax.psum(owned_rows, 'head').astype(jnp.float32)]
    all_gather x0 -> x1, blocking collectives: none -> 29.1 us  [on_device(): lax.all_gather(owned_rows, 'head')]
    reduce_scatter x1, waiting for transfers between devices: 117 us -> 111 us  [on_device(): lax.psum_scatter(latent_grad.astype(jnp.bfloat16), 'leaf', scatter_dimens...]
  transfers between devices with their start and end apart: 3 -> 2, of which waited for: 3 -> 2; matrix products, arithmetic and copies ran while one was open for 5% -> 6% of each run, Pallas kernels for 0% -> 0%
where the time goes in v1:
time: 271 us; the launch traced here: 270 us
  waiting for transfers between devices  184 us (68%)
  matrix products  33.7 us (12%)
  blocking collectives  29.1 us (11%)
  between operations  14.3 us (5%)
  other arithmetic  5.09 us (2%)
  local copies, waits for them, and re-layouts  3.47 us (1%)
    reduce_scatter x1, waiting for transfers between devices, on_device(): lax.psum_scatter(latent_grad.astype(jnp.bfloat16), 'leaf', scatter_dimens...  111 us
    all_gather x1, waiting for transfers between devices, on_device(): backward_block_keys = lax.all_gather(latents, 'leaf', axis=0, tiled=True)  72.7 us
    all_gather x1, blocking collectives, on_device(): lax.all_gather(owned_rows, 'head')  29.1 us
    dot_general x1, matrix products, advance(): jnp.einsum('thc,kc->thk', grad_latent, backward_block_keys, preferred_ele...  5.48 us
    dot_general x1, matrix products, on_device(): jnp.einsum('thc,hdc->thd', query_grad, key_up_matrix, preferred_element_t...  5.47 us
  transfers between devices with their start and end apart: 2, of which 2 were waited for; matrix products, arithmetic and copies ran while one was open for 6% of the time, Pallas kernels for 0%

profile of v1, /device:TPU:4, one launch (start us, length us, event | category | flops | bytes accessed | tf_op | source)
XLA Modules:
  0.0 269.9 jit_solution(2311044595271952033)
XLA Ops:
  7.2 0.7 all-gather.3.cloned.1.call-update
  8.0 0.8 reduce-window.8
  8.8 0.1 convert_reduce_fusion
  8.9 0.7 select_reduce_fusion
  9.6 1.0 convolution_minimum_fusion.8
  10.7 0.4 convolution_minimum_fusion.7
  11.1 0.4 convolution_minimum_fusion.6
  11.4 0.4 convolution_minimum_fusion.5
  11.8 0.4 convolution_minimum_fusion.4
  12.2 0.4 convolution_minimum_fusion.3
  12.6 0.4 convolution_minimum_fusion.2
  13.0 0.4 convolution_minimum_fusion.1
  13.4 0.4 convolution_minimum_fusion
  13.8 0.3 convolution_compare_fusion
  14.0 0.1 copy.34
  14.2 0.1 broadcast_bitcast_fusion
  14.3 0.4 copy.35
  14.7 1.5 fusion.23
  16.2 2.4 fusion.24
  18.6 72.7 %all-gather.3.cloned.1.call-done = bf16[2048,512]{1,0:T(8,128)(2,1)} async-done(((bf16[64,512]{1,0:T(8,128)(2,1)}), bf16[2048,512]{1,0:T(8,128)(2,1)}) %all-gather.3.cloned.1.call-update) | async-done | bytes 2097168 | tf_op jit(solution)/shard_map/all_gather | solution.py:91
  91.3 4.5 %fusion.3 = (f32[128,8]{0,1:T(8,128)S(1)}, f32[128,8,2048]{2,0,1:T(8,128)S(1)}) fusion(pred[128,2048]{1,0:T(8,128)(4,1)S(1)} %copy.35, bf16[128,8,512]{0,2,1:T(8,128)(2,1)S(1)} %fusion.23, bf16[2048,512]{1,0:T(8,128)(2,1)} %all-gather.3.cloned.1.call-done), kind=kOutput, calls=%fused_computation.7 | convolution fusion | flops 2153774080 | bytes 11800576 | tf_op jit(solution)/shard_map/thc,kc->thk/dot_general | solution.py:58
  95.8 2.7 fusion.1
  98.5 3.3 %fusion.4 = f32[2048,512,1]{1,0,2:T(8,128)S(1)} fusion(bf16[128,8,512]{0,2,1:T(8,128)(2,1)S(1)} %copy-done.2, f32[128,8,2048]{2,0,1:T(8,128)S(1)} %get-tuple-element.9, f32[128,8]{0,1:T(8,128)S(1)} %log_add_fusion, pred[128,2048]{1,0:T(8,128)(4,1)S(1)} %copy.35), kind=kOutput, calls=%fused_computation.8 | convolution fusion | flops 2157969408 | bytes 13897728 | tf_op jit(solution)/shard_map/thk,thc->kc/dot_general | solution.py:106
  101.8 2.8 %multiply_reduce_fusion = f32[128,8]{0,1:T(8,128)S(1)} fusion(bf16[128,8,512]{0,2,1:T(8,128)(2,1)S(1)} %copy-done.2, f32[128,8]{0,1:T(8,128)S(1)} %fusion.1, bf16[2048,512]{1,0:T(8,128)(2,1)S(1)} %copy-done.3, f32[128,8,2048]{2,0,1:T(8,128)S(1)} %get-tuple-element.9, f32[128,8]{0,1:T(8,128)S(1)} %broadcast_maximum_fusion, pred[128,2048]{1,0:T(8,128)(4,1)S(1)} %copy.35), kind=kOutput, calls=%fused_computation.26 | convolution fusion | flops 2160065536 | bytes 11808768 | tf_op jit(solution)/shard_map/thk,kc->thc/dot_general | solution.py:75
  104.6 5.5 %multiply_convert_fusion = bf16[128,8,2048]{2,0,1:T(8,128)(2,1)S(1)} fusion(f32[128,8,2048]{2,0,1:T(8,128)S(1)} %get-tuple-element.9, f32[128,8]{0,1:T(8,128)S(1)} %multiply_reduce_fusion, f32[128,8]{0,1:T(8,128)S(1)} %log_add_fusion, pred[128,2048]{1,0:T(8,128)(4,1)S(1)} %copy.35, bf16[128,8,512]{0,2,1:T(8,128)(2,1)S(1)} %copy-done.2, ...), kind=kOutput, calls=%fused_computation | convolution fusion | flops 2162163712 | bytes 15998976 | tf_op jit(solution)/shard_map/thc,kc->thk/dot_general | solution.py:96
  110.1 1.9 copy-done.4
  112.0 4.0 %fusion.6 = bf16[2048,512]{1,0:T(8,128)(2,1)} fusion(f32[2048,512,1]{1,0,2:T(8,128)S(1)} %fusion.4, bf16[128,8,2048]{2,0,1:T(8,128)(2,1)S(1)} %multiply_convert_fusion, bf16[128,8,512]{0,2,1:T(8,128)(2,1)S(1)} %fusion.23), kind=kOutput, calls=%fused_computation.10 | convolution fusion | flops 2150629376 | bytes 11534336 | tf_op jit(solution)/shard_map/thk,thc->kc/dot_general | solution.py:103
  116.0 5.5 %fusion.31 = bf16[128,8,128]{2,0,1:T(8,128)(2,1)S(1)} fusion(bf16[8,128,512]{2,1,0:T(8,128)(2,1)S(1)} %copy-done, bf16[128,8,2048]{2,0,1:T(8,128)(2,1)} %copy-done.4, bf16[2048,512]{1,0:T(8,128)(2,1)} %all-gather.3.cloned.1.call-done), kind=kOutput, calls=%fused_computation.42 | convolution fusion | flops 2282881024 | bytes 7602176 | tf_op jit(solution)/shard_map/thc,hdc->thd/dot_general | solution.py:116
  121.5 0.9 copy.46
  122.4 110.9 %reduce-scatter.2.cloned.1.call-done = bf16[64,512]{1,0:T(8,128)(2,1)} async-done(((bf16[2048,512]{1,0:T(8,128)(2,1)}), bf16[64,512]{1,0:T(8,128)(2,1)}) %reduce-scatter.2.cloned.1.call-update) | async-done | bytes 65552 | tf_op jit(solution)/shard_map/reduce_scatter | solution.py:119
  233.3 29.1 %all-gather = bf16[512,512]{1,0:T(8,128)(2,1)S(1)} all-gather(bf16[64,512]{1,0:T(8,128)(2,1)} %reduce-scatter.2.cloned.1.call-done), channel_id=2, replica_groups=mesh['leaf'=32,'head'=8] {'head'}, dimensions={0}, use_global_device_ids=true | all-gather | bytes 589824 | tf_op jit(solution)/shard_map/all_gather | solution.py:122
  262.4 0.7 convert_element_type.59
  (15 shorter events, 0.2 us)
Async XLA Ops:
  7.2 7.6 %copy-start = (bf16[8,128,512]{2,1,0:T(8,128)(2,1)S(1)}, bf16[8,128,512]{2,1,0:T(8,128)(2,1)}, u32[]{:S(2)}) copy-start(bf16[8,128,512]{2,1,0:T(8,128)(2,1)} %param.11) | copy-start | bytes 3145732
  7.2 9.0 %copy-start.1 = (bf16[8,512,128]{2,1,0:T(8,128)(2,1)S(1)}, bf16[8,512,128]{2,1,0:T(8,128)(2,1)}, u32[]{:S(2)}) copy-start(bf16[8,512,128]{2,1,0:T(8,128)(2,1)} %param.12) | copy-start | bytes 3145732
  7.2 84.1 %all-gather.3.cloned.1.call-start = ((), (), s32[]{:S(2)}) async-start(), calls=%async_computation.1 | async-start | bytes 2162688 | tf_op jit(solution)/shard_map/all_gather | solution.py:91
  7.9 225.3 %reduce-scatter.2.cloned.1.call-start = ((), (), s32[]{:S(2)}) async-start(), calls=%async_computation.2 | async-start | bytes 2162688 | tf_op jit(solution)/shard_map/reduce_scatter | solution.py:119
  18.6 79.9 %copy-start.2 = (bf16[128,8,512]{0,2,1:T(8,128)(2,1)S(1)}, bf16[128,8,512]{0,2,1:T(8,128)(2,1)}, u32[]{:S(2)}) copy-start(bf16[128,8,512]{0,2,1:T(8,128)(2,1)} %fusion.24) | copy-start | bytes 3145732
  98.5 3.3 %copy-start.3 = (bf16[2048,512]{1,0:T(8,128)(2,1)S(1)}, bf16[2048,512]{1,0:T(8,128)(2,1)}, u32[]{:S(2)}) copy-start(bf16[2048,512]{1,0:T(8,128)(2,1)} %all-gather.3.cloned.1.call-done) | copy-start | bytes 6291460
  110.1 1.9 copy-start.4
Sparse Core Ops, SparseCore 0:
  10.8 80.4 all-gather.2
  116.2 117.0 reduce-scatter.1
